TPU v7x, 256 devices: a whole 4x4x8 slice. The times are simulated.
256 devices in a mesh: blk: 32 (over z, y_lo, core), chan: 8 (over y_hi, x).
Axes of the slice: x: 4, y: 4 (y_hi: 2, y_lo: 2; y = y_hi * 2 + y_lo), z: 8, core: 2. Of those that a mesh axis runs over, the one named last changes fastest.
Arguments:
- spec_in: bfloat16 [256, 2, 512, 128], P('chan', None, 'blk'), may hold values from -6 to 6
- weight: bfloat16 [128, 2, 256, 256], P('blk', None, 'chan'), may hold values from -0.5 to 0.5
- pattern: int32 [128, 4, 4], P('blk'), may hold values 0 or 1
- cotangent: bfloat16 [256, 2, 512, 128], P('chan', None, 'blk'), may hold values from -6 to 6
Outputs:
- spec_out: bfloat16 [256, 2, 512, 128], P('chan', None, 'blk')
- grad_in: bfloat16 [256, 2, 512, 128], P('chan', None, 'blk')
- grad_weight: float32 [128, 2, 256, 256], P('blk', None, 'chan')
All inputs are finite; a program needn't handle non-finite values. No bound on the sum of `pattern` on one device may be relied on, other than what follows from the above.
Results may differ from a plain program's by a relative error of at most 0.001.
Values may be sent and summed in bfloat16 or wider, within the bound.
A program may use at most 128 MiB of HBM per device.

v0:
```python
import jax
import jax.numpy as jnp
from jax import lax
from jax.sharding import PartitionSpec as P


def mix_forward(x_real, x_imag, w_real, w_imag):
    form = "ism,mio->osm"
    real_part = jnp.einsum(form, x_real, w_real, preferred_element_type=jnp.float32) - jnp.einsum(
        form, x_imag, w_imag, preferred_element_type=jnp.float32
    )
    imag_part = jnp.einsum(form, x_real, w_imag, preferred_element_type=jnp.float32) + jnp.einsum(
        form, x_imag, w_real, preferred_element_type=jnp.float32
    )
    return jnp.stack([real_part, imag_part], axis=1)


def mix_input_grad(g_real, g_imag, w_real, w_imag):
    form = "osm,mio->ism"
    real_part = jnp.einsum(form, g_real, w_real, preferred_element_type=jnp.float32) + jnp.einsum(
        form, g_imag, w_imag, preferred_element_type=jnp.float32
    )
    imag_part = jnp.einsum(form, g_imag, w_real, preferred_element_type=jnp.float32) - jnp.einsum(
        form, g_real, w_imag, preferred_element_type=jnp.float32
    )
    return jnp.stack([real_part, imag_part], axis=1)


def mix_weight_grad(x_real, x_imag, g_real, g_imag):
    form = "ism,osm->mio"
    real_part = jnp.einsum(form, x_real, g_real, preferred_element_type=jnp.float32) + jnp.einsum(
        form, x_imag, g_imag, preferred_element_type=jnp.float32
    )
    imag_part = jnp.einsum(form, x_real, g_imag, preferred_element_type=jnp.float32) - jnp.einsum(
        form, x_imag, g_real, preferred_element_type=jnp.float32
    )
    return jnp.stack([real_part, imag_part], axis=1)


def local(spec_in, weight, pattern, cotangent):
    in_rows = spec_in.shape[0]
    width = weight.shape[3]
    block_size = width // pattern.shape[2]
    full_mask = jnp.repeat(
        jnp.repeat(pattern.astype(jnp.bfloat16), block_size, axis=1), block_size, axis=2
    )
    own_mask = lax.dynamic_slice_in_dim(full_mask, lax.axis_index("chan") * in_rows, in_rows, 1)
    masked = weight * own_mask[:, None]
    full_weight = lax.all_gather(masked, "blk", axis=0, tiled=True)
    x_real = spec_in[:, 0]
    x_imag = spec_in[:, 1]
    grad_full = lax.all_gather(cotangent, "chan", axis=0, tiled=True)
    w_real = full_weight[:, 0]
    w_imag = full_weight[:, 1]
    summed = lax.psum_scatter(
        mix_forward(x_real, x_imag, w_real, w_imag), "chan", scatter_dimension=0, tiled=True
    )
    spec_out = summed.astype(jnp.bfloat16)
    grad_in = mix_input_grad(grad_full[:, 0], grad_full[:, 1], w_real, w_imag).astype(jnp.bfloat16)
    gs_real = grad_full[:, 0]
    gs_imag = grad_full[:, 1]
    weight_sum = lax.psum_scatter(
        mix_weight_grad(x_real, x_imag, gs_real, gs_imag), "blk", scatter_dimension=0, tiled=True
    )
    grad_weight = weight_sum * own_mask[:, None].astype(jnp.float32)
    return (spec_out, grad_in, grad_weight)


def solution(mesh):
    in_specs = (
        P("chan", None, "blk", None),
        P("blk", None, "chan", None),
        P("blk", None, None),
        P("chan", None, "blk", None),
    )
    out_specs = (
        P("chan", None, "blk", None),
        P("chan", None, "blk", None),
        P("blk", None, "chan", None),
    )
    return jax.shard_map(local, mesh=mesh, in_specs=in_specs, out_specs=out_specs, check_vma=False)
```

profile of v0, /device:TPU:2, one launch (start us, length us, event | category | flops | bytes accessed | tf_op | source)
XLA Modules:
  0.0 498.5 jit_solution(17210475181012896570)
XLA Ops:
  7.2 0.0 all-gather.5.cloned.1.call-start
  7.2 0.7 all-gather.5.cloned.1.call-update
  7.9 0.0 all-gather.3.cloned.1.call-start
  7.9 0.7 convert_element_type.11
  8.7 0.1 copy.36
  8.8 0.1 broadcast_in_dim.8
  8.9 0.1 reshape.15
  9.0 0.1 constant_dynamic-slice_fusion
  9.2 0.1 copy.50
  9.3 1.6 copy_multiply_fusion
  10.9 0.0 all-gather.3.cloned.1.call-update
  10.9 0.0 all-reduce.3.cloned.1.call-start
  10.9 1.0 fusion.27
  11.9 0.5 copy.49
  12.4 0.5 copy.51
  12.9 60.5 %all-gather.5.cloned.1.call-done = bf16[256,2,16,128]{3,2,1,0:T(8,128)(2,1)} async-done(((bf16[32,2,16,128]{3,2,1,0:T(8,128)(2,1)}), bf16[256,2,16,128]{3,2,1,0:T(8,128)(2,1)}) %all-gather.5.cloned.1.call-update) | async-done | bytes 2097168 | tf_op jit(solution)/shard_map/all_gather | solution.py:52
  73.4 2.9 fusion.26
  76.3 1.3 copy.52
  77.5 2.2 copy.53
  79.7 0.8 fusion.14
  80.5 0.8 add_bitcast_fusion
  81.3 0.8 fusion.8
  82.1 0.8 subtract_bitcast_fusion
  82.9 4.1 pad_maximum_fusion
  87.1 0.0 all-reduce.3.cloned.1.call-update
  87.1 0.2 reduce-scatter.5.cloned.1.call-start
  87.3 54.5 %all-gather.3.cloned.1.call-done = bf16[128,2,32,256]{3,2,0,1:T(8,128)(2,1)} async-done(((bf16[4,2,32,256]{3,2,0,1:T(8,128)(2,1)}), bf16[128,2,32,256]{3,2,0,1:T(8,128)(2,1)}) %all-gather.3.cloned.1.call-update) | async-done | bytes 4194320 | tf_op jit(solution)/shard_map/all_gather | solution.py:49
  141.8 0.0 copy-start
  141.8 2.2 fusion.2
  144.0 0.7 copy-done
  144.6 0.5 subtract_bitcast_fusion.1
  145.1 0.4 fusion.3
  145.6 0.5 add_bitcast_fusion.1
  146.1 2.4 pad_maximum_fusion.1
  148.5 5.8 %copy.41 = f32[256,2,16,128]{3,2,1,0:T(8,128)} copy(f32[256,2,16,128]{0,2,3,1:T(8,128)} %pad_maximum_fusion.1) | data formatting | bytes 8388608 | tf_op jit(solution)/shard_map/stack | solution.py:15
  154.3 0.0 copy-start.3
  154.3 0.0 reduce-scatter.5.cloned.1.call-update
  154.3 0.6 copy-done.3
  155.0 0.6 dynamic-slice
  156.2 0.0 copy-start.1
  156.2 2.4 fusion.1
  158.6 0.4 copy-done.1
  159.0 0.7 fusion.7
  159.7 0.5 copy.44
  160.2 0.0 copy-start.2
  160.2 2.4 fusion
  162.7 0.5 copy-done.2
  163.1 0.7 fusion.6
  163.8 0.5 copy.45
  164.4 0.7 pad_maximum_fusion.2
  165.1 231.4 %all-reduce.3.cloned.1.call-done = f32[128,2,32,256]{3,2,0,1:T(8,128)} async-done(((f32[128,2,32,256]{3,2,0,1:T(8,128)}), f32[128,2,32,256]{3,2,0,1:T(8,128)}) %all-reduce.3.cloned.1.call-update) | async-done | bytes 8388624
  396.5 1.0 dynamic-slice_multiply_fusion
  397.4 0.7 copy.46
  398.2 92.0 %reduce-scatter.5.cloned.1.call-done = f32[32,2,16,128]{3,2,1,0:T(8,128)} async-done(((f32[256,2,16,128]{3,2,1,0:T(8,128)}), f32[32,2,16,128]{3,2,1,0:T(8,128)}) %reduce-scatter.5.cloned.1.call-update) | async-done | bytes 524304 | tf_op jit(solution)/shard_map/reduce_scatter | solution.py:55
  490.2 1.8 convert_element_type.12
  (2 shorter events, 0.1 us)
Async XLA Ops:
  7.2 66.2 %all-gather.5.cloned.1.call-start = ((), (), s32[]{:S(2)}) async-start(), calls=%async_computation.3 | async-start | bytes 2359296 | tf_op jit(solution)/shard_map/all_gather | solution.py:52
  7.9 133.9 %all-gather.3.cloned.1.call-start = ((), (), s32[]{:S(2)}) async-start(), calls=%async_computation.1 | async-start | bytes 4325376 | tf_op jit(solution)/shard_map/all_gather | solution.py:49
  10.9 385.6 %all-reduce.3.cloned.1.call-start = ((), (), s32[]{:S(2)}) async-start(), calls=%async_computation.4 | async-start | bytes 16777216
  87.1 403.1 %reduce-scatter.5.cloned.1.call-start = ((), (), s32[]{:S(2)}) async-start(), calls=%async_computation.2 | async-start | bytes 4718592 | tf_op jit(solution)/shard_map/reduce_scatter | solution.py:55
  141.8 2.8 copy-start
  154.3 0.7 copy-start.3
  156.2 2.8 copy-start.1
  160.2 2.9 copy-start.2
Sparse Core Ops, SparseCore 0:
  10.6 62.7 all-gather.4
  75.8 65.9 all-gather.2
  144.5 251.9 all-reduce.2
  400.5 89.6 reduce-scatter.4
where the time goes:
time: 499 us; the launch traced here: 498 us
  waiting for transfers between devices  439 us (88%)
  local copies, waits for them, and re-layouts  19.2 us (4%)
  between operations  14.6 us (3%)
  matrix products  13 us (3%)
  other arithmetic  12.3 us (2%)
    unnamed x5, waiting for transfers between devices  232 us
    reduce_scatter x1, waiting for transfers between devices, local(): lax.psum_scatter(mix_forward(x_real, x_imag, w_real, w_imag), 'chan', sca...  92 us
    all_gather x1, waiting for transfers between devices, local(): grad_full = lax.all_gather(cotangent, 'chan', axis=0, tiled=True)  60.5 us
    all_gather x1, waiting for transfers between devices, local(): full_weight = lax.all_gather(masked, 'blk', axis=0, tiled=True)  54.5 us
  transfers between devices with their start and end apart: 4, of which 4 were waited for; matrix products, arithmetic and copies ran while one was open for 8% of the time, Pallas kernels for 0%

commit v1 on v0

--- a/solution.py
+++ b/solution.py
@@ -49,7 +49,9 @@
     full_weight = lax.all_gather(masked, "blk", axis=0, tiled=True)
     x_real = spec_in[:, 0]
     x_imag = spec_in[:, 1]
-    grad_full = lax.all_gather(cotangent, "chan", axis=0, tiled=True)
+    grad_full = jnp.concatenate(
+        lax.all_to_all(jnp.stack([cotangent] * lax.axis_size("chan")), "chan", 0, 0), axis=0
+    )
     w_real = full_weight[:, 0]
     w_imag = full_weight[:, 1]
     summed = lax.psum_scatter(

time: 499 us -> 451 us (0.904)
  waiting for transfers between devices: 439 us -> 382 us
  starting transfers between devices: 0.34 us -> 7.72 us
    all_gather x1 -> x0, waiting for transfers between devices: 60.5 us -> none  [local(): grad_full = lax.all_gather(cotangent, 'chan', axis=0, tiled=True)]
    all_to_all x0 -> x1, waiting for transfers between devices: none -> 26.3 us  [local(): lax.all_to_all(jnp.stack([cotangent] * lax.axis_size('chan')), 'chan', 0, 0)]
    all_gather x1, waiting for transfers between devices: 54.5 us -> 32.9 us  [local(): full_weight = lax.all_gather(masked, 'blk', axis=0, tiled=True)]
    all_to_all x0 -> x1, starting transfers between devices: none -> 7.46 us  [local(): lax.all_to_all(jnp.stack([cotangent] * lax.axis_size('chan')), 'chan', 0, 0)]
    unnamed x5 -> x4, waiting for transfers between devices: 232 us -> 231 us
  transfers between devices with their start and end apart: 4 -> 4, of which waited for: 4 -> 4; matrix products, arithmetic and copies ran while one was open for 8% -> 9% of each run, Pallas kernels for 0% -> 0%
where the time goes in v1:
time: 451 us; the launch traced here: 450 us
  waiting for transfers between devices  382 us (85%)
  local copies, waits for them, and re-layouts  20.6 us (5%)
  between operations  14.6 us (3%)
  matrix products  13 us (3%)
  other arithmetic  12.3 us (3%)
  starting transfers between devices  7.72 us (2%)
    unnamed x4, waiting for transfers between devices  231 us
    reduce_scatter x1, waiting for transfers between devices, local(): lax.psum_scatter(mix_forward(x_real, x_imag, w_real, w_imag), 'chan', sca...  92.1 us
    all_gather x1, waiting for transfers between devices, local(): full_weight = lax.all_gather(masked, 'blk', axis=0, tiled=True)  32.9 us
    all_to_all x1, waiting for transfers between devices, local(): lax.all_to_all(jnp.stack([cotangent] * lax.axis_size('chan')), 'chan', 0, 0)  26.3 us
  transfers between devices with their start and end apart: 4, of which 4 were waited for; matrix products, arithmetic and copies ran while one was open for 9% of the time, Pallas kernels for 0%

profile of v1, /device:TPU:2, one launch (start us, length us, event | category | flops | bytes accessed | tf_op | source)
XLA Modules:
  0.0 450.2 jit_solution(7479486170120768969)
XLA Ops:
  7.2 0.0 all-gather.2.cloned.1.call-start
  7.2 0.7 convert_element_type.11
  7.9 0.1 copy.37
  8.0 0.1 broadcast_in_dim.8
  8.1 0.1 reshape.20
  8.2 0.0 copy-start.3
  8.3 0.1 constant_dynamic-slice_fusion
  8.4 0.1 copy.51
  8.5 1.6 copy_multiply_fusion
  10.1 0.0 all-gather.2.cloned.1.call-update
  10.1 2.6 stack.44
  12.8 7.5 %all-to-all-start = ((bf16[8,32,2,16,128]{4,3,2,1,0:T(8,128)(2,1)}), bf16[8,32,2,16,128]{4,3,2,1,0:T(8,128)(2,1)S(1)}, u32[]{:S(2)}, u32[]{:S(2)}) async-start(bf16[8,32,2,16,128]{4,3,2,1,0:T(8,128)(2,1)} %stack.44), calls=%async_computation.1 | async-start | bytes 4194304 | tf_op jit(solution)/shard_map/all_to_all | solution.py:53
  20.2 0.0 all-reduce.3.cloned.1.call-start
  20.2 0.0 copy-done.3
  20.3 0.5 copy.50
  20.8 0.5 copy.52
  21.2 26.3 %all-to-all-done = bf16[8,32,2,16,128]{4,3,2,1,0:T(8,128)(2,1)S(1)} async-done(((bf16[8,32,2,16,128]{4,3,2,1,0:T(8,128)(2,1)}), bf16[8,32,2,16,128]{4,3,2,1,0:T(8,128)(2,1)S(1)}, u32[]{:S(2)}, u32[]{:S(2)}) %all-to-all-start) | async-done | bytes 2097184 | tf_op jit(solution)/shard_map/all_to_all | solution.py:53
  47.6 1.7 fusion.26
  49.3 2.2 copy.53
  51.5 2.2 copy.54
  53.7 0.8 fusion.14
  54.5 0.8 add_bitcast_fusion
  55.3 0.8 fusion.8
  56.1 0.8 subtract_bitcast_fusion
  56.9 4.1 pad_maximum_fusion
  61.0 0.0 all-reduce.3.cloned.1.call-update
  61.0 0.2 reduce-scatter.5.cloned.1.call-start
  61.3 32.9 %all-gather.2.cloned.1.call-done = bf16[128,2,32,256]{3,2,0,1:T(8,128)(2,1)} async-done(((bf16[4,2,32,256]{3,2,0,1:T(8,128)(2,1)}), bf16[128,2,32,256]{3,2,0,1:T(8,128)(2,1)}) %all-gather.2.cloned.1.call-update) | async-done | bytes 4194320 | tf_op jit(solution)/shard_map/all_gather | solution.py:49
  94.2 0.0 copy-start
  94.2 2.2 fusion.2
  96.4 0.7 copy-done
  97.0 0.5 subtract_bitcast_fusion.1
  97.5 0.4 fusion.3
  97.9 0.5 add_bitcast_fusion.1
  98.5 2.4 pad_maximum_fusion.1
  100.9 5.8 %copy.42 = f32[256,2,16,128]{3,2,1,0:T(8,128)} copy(f32[256,2,16,128]{0,2,3,1:T(8,128)} %pad_maximum_fusion.1) | data formatting | bytes 8388608 | tf_op jit(solution)/shard_map/stack | solution.py:15
  106.7 0.0 copy-start.4
  106.7 0.0 reduce-scatter.5.cloned.1.call-update
  106.7 0.6 copy-done.4
  107.4 0.6 dynamic-slice
  108.6 0.0 copy-start.1
  108.6 2.4 fusion.1
  111.0 0.4 copy-done.1
  111.4 0.7 fusion.7
  112.1 0.5 copy.45
  112.6 0.0 copy-start.2
  112.6 2.4 fusion
  115.1 0.5 copy-done.2
  115.6 0.7 fusion.6
  116.3 0.5 copy.46
  116.8 0.7 pad_maximum_fusion.2
  117.5 230.5 %all-reduce.3.cloned.1.call-done = f32[128,2,32,256]{3,2,0,1:T(8,128)} async-done(((f32[128,2,32,256]{3,2,0,1:T(8,128)}), f32[128,2,32,256]{3,2,0,1:T(8,128)}) %all-reduce.3.cloned.1.call-update) | async-done | bytes 8388624
  348.0 1.0 dynamic-slice_multiply_fusion
  349.0 0.7 copy.47
  349.7 92.1 %reduce-scatter.5.cloned.1.call-done = f32[32,2,16,128]{3,2,1,0:T(8,128)} async-done(((f32[256,2,16,128]{3,2,1,0:T(8,128)}), f32[32,2,16,128]{3,2,1,0:T(8,128)}) %reduce-scatter.5.cloned.1.call-update) | async-done | bytes 524304 | tf_op jit(solution)/shard_map/reduce_scatter | solution.py:57
  441.9 1.8 convert_element_type.12
  (3 shorter events, 0.1 us)
Async XLA Ops:
  7.2 87.0 %all-gather.2.cloned.1.call-start = ((), (), s32[]{:S(2)}) async-start(), calls=%async_computation.2 | async-start | bytes 4325376 | tf_op jit(solution)/shard_map/all_gather | solution.py:49
  8.2 12.0 %copy-start.3 = (bf16[32,2,16,128]{3,2,1,0:T(8,128)(2,1)S(1)}, bf16[32,2,16,128]{3,2,1,0:T(8,128)(2,1)}, u32[]{:S(2)}) copy-start(bf16[32,2,16,128]{3,2,1,0:T(8,128)(2,1)} %param.4) | copy-start | bytes 786436
  12.8 34.8 %all-to-all-start = ((bf16[8,32,2,16,128]{4,3,2,1,0:T(8,128)(2,1)}), bf16[8,32,2,16,128]{4,3,2,1,0:T(8,128)(2,1)S(1)}, u32[]{:S(2)}, u32[]{:S(2)}) async-start(bf16[8,32,2,16,128]{4,3,2,1,0:T(8,128)(2,1)} %stack.44), calls=%async_computation.1 | async-start | bytes 4194304 | tf_op jit(solution)/shard_map/all_to_all | solution.py:53
  20.2 327.8 %all-reduce.3.cloned.1.call-start = ((), (), s32[]{:S(2)}) async-start(), calls=%async_computation.4 | async-start | bytes 16777216
  61.0 380.8 %reduce-scatter.5.cloned.1.call-start = ((), (), s32[]{:S(2)}) async-start(), calls=%async_computation.3 | async-start | bytes 4718592 | tf_op jit(solution)/shard_map/reduce_scatter | solution.py:57
  94.2 2.8 copy-start
  106.7 0.7 copy-start.4
  108.6 2.8 copy-start.1
  112.6 2.9 copy-start.2
Sparse Core Ops, SparseCore 0:
  10.4 83.7 all-gather.1
  96.9 251.1 all-reduce.2
  352.2 89.6 reduce-scatter.4
